TPU v7x, 32 devices: a whole 2x2x4 slice. The times are simulated.
32 devices in a mesh: seq: 2 (over x), fsdp: 16 (over z, y, core).
Axes of the slice: x: 2, y: 2, z: 4, core: 2. Of those that a mesh axis runs over, the one named last changes fastest.
Arguments:
- tokens: bfloat16 [16, 1024, 768], P('fsdp', 'seq'), may hold values from -6 to 6
- prior_logits: bfloat16 [16, 12, 1024, 1024], P('fsdp', 'seq'), may hold values from -6 to 6
- lengths: int32 [16], P('fsdp'), may hold values from 256 to 1024, as said below
- order: int32 [16, 1024], P('fsdp'), may hold values from 0 to 1023, each once within a row
- cotangent: bfloat16 [16, 1024, 768], P('fsdp', 'seq'), may hold values from -6 to 6
- w_qkv: bfloat16 [768, 2304], P('fsdp'), may hold values from -0.21875 to 0.21875
- w_out: bfloat16 [768, 768], P('fsdp'), may hold values from -3.5 to 3.5
- w_in: bfloat16 [768, 3072], P('fsdp'), may hold values from -0.21875 to 0.21875
- w_back: bfloat16 [3072, 768], P('fsdp'), may hold values from -0.109375 to 0.109375
- bias_q: bfloat16 [768], P('fsdp'), may hold values from -1.5 to 1.5
- bias_v: bfloat16 [768], P('fsdp'), may hold values from -0.25 to 0.25
- bias_o: bfloat16 [768], P('fsdp'), may hold values from -1.5 to 1.5
- gain_one: bfloat16 [768], P('fsdp'), may hold values from 0.5 to 1.5
- shift_one: bfloat16 [768], P('fsdp'), may hold values from -1.5 to 1.5
- bias_in: bfloat16 [3072], P('fsdp'), may hold values from -1.5 to 1.5
- bias_back: bfloat16 [768], P('fsdp'), may hold values from -1.5 to 1.5
- gain_two: bfloat16 [768], P('fsdp'), may hold values from 0.5 to 1.5
- shift_two: bfloat16 [768], P('fsdp'), may hold values from -1.5 to 1.5
Outputs:
- output: bfloat16 [16, 1024, 768], P('fsdp', 'seq')
- raw_logits: bfloat16 [16, 12, 1024, 1024], P('fsdp', 'seq')
- tokens_grad: bfloat16 [16, 1024, 768], P('fsdp', 'seq')
- prior_grad: bfloat16 [16, 12, 1024, 1024], P('fsdp', 'seq')
- grad_w_qkv: float32 [768, 2304], P('fsdp')
- grad_w_out: float32 [768, 768], P('fsdp')
- grad_w_in: float32 [768, 3072], P('fsdp')
- grad_w_back: float32 [3072, 768], P('fsdp')
- grad_bias_q: float32 [768], P('fsdp')
- grad_bias_v: float32 [768], P('fsdp')
- grad_bias_o: float32 [768], P('fsdp')
- grad_gain_one: float32 [768], P('fsdp')
- grad_shift_one: float32 [768], P('fsdp')
- grad_bias_in: float32 [3072], P('fsdp')
- grad_bias_back: float32 [768], P('fsdp')
- grad_gain_two: float32 [768], P('fsdp')
- grad_shift_two: float32 [768], P('fsdp')
- rms: float32 [3], replicated
Inputs may be any that keep to these rules, and one draw needn't show every extreme that they name: `lengths`: positions below a sequence's length hold its tokens, the others are padding; some sequence has exactly 1024.
All inputs are finite; a program needn't handle non-finite values.
Results may differ from a plain program's by a relative error of at most 0.017.
Values may be sent and summed in bfloat16 or wider, within the bound.
No kernel may reach another device: no remote copies, remote signals or barrier semaphores. Data moves between devices by JAX's collectives and lax.ppermute only.
A program may use at most 192 MiB of HBM per device.

v0:
```python
import math
import jax
import jax.numpy as jnp
from jax import lax
from jax.sharding import PartitionSpec as P

HD = 64
eps_norm = 1e-05
masked_fill = -1e30


def layer_norm(values, gain, shift):
    average = jnp.mean(values, axis=-1, keepdims=True)
    centered = values - average
    variance = jnp.mean(centered * centered, axis=-1, keepdims=True)
    return centered * lax.rsqrt(variance + eps_norm) * gain + shift


def gelu_exact(values):
    return jax.nn.gelu(values, approximate=False)


def contract_rows(left, right):
    return lax.dot_general(
        left, right, (((0,), (0,)), ((), ())), preferred_element_type=jnp.float32
    )


def contract_cols(left, right):
    return lax.dot_general(
        left, right, (((1,), (1,)), ((), ())), preferred_element_type=jnp.float32
    )


def body(
    tokens,
    prior_logits,
    lengths,
    order,
    cotangent,
    w_qkv,
    w_out,
    w_in,
    w_back,
    bias_q,
    bias_v,
    bias_o,
    gain_one,
    shift_one,
    bias_in,
    bias_back,
    gain_two,
    shift_two,
):
    seq_count = lax.axis_size("seq")
    seq_index = lax.axis_index("seq")
    qkv_weight, proj_weight, query_bias, value_bias, proj_bias, first_gain, first_shift = (
        lax.all_gather(w_qkv, "fsdp", axis=0, tiled=True),
        lax.all_gather(w_out, "fsdp", axis=0, tiled=True),
        lax.all_gather(bias_q, "fsdp", axis=0, tiled=True),
        lax.all_gather(bias_v, "fsdp", axis=0, tiled=True),
        lax.all_gather(bias_o, "fsdp", axis=0, tiled=True),
        lax.all_gather(gain_one, "fsdp", axis=0, tiled=True),
        lax.all_gather(shift_one, "fsdp", axis=0, tiled=True),
    )
    rows = tokens[0]
    local_count = rows.shape[0]
    width = rows.shape[1]
    heads_local = prior_logits.shape[1]
    local_width = heads_local * HD
    total = local_count * seq_count
    scale = 1.0 / math.sqrt(HD)
    joint_bias = jnp.concatenate(
        [
            query_bias.astype(jnp.float32),
            jnp.zeros((width,), jnp.float32),
            value_bias.astype(jnp.float32),
        ]
    )
    joint = (jnp.dot(rows, qkv_weight, preferred_element_type=jnp.float32) + joint_bias).astype(
        jnp.bfloat16
    )
    joint = joint.reshape(local_count, 3, seq_count, local_width)
    headed = lax.all_to_all(joint, "seq", split_axis=2, concat_axis=0, tiled=True).reshape(
        total, 3, local_width
    )
    order_row = order[0]
    length = lengths[0]
    positions = jnp.arange(total, dtype=jnp.int32)
    inverse = jnp.zeros((total,), jnp.int32).at[order_row].set(positions)
    placed = headed[inverse]
    query_pos = placed[:, 0].reshape(total, heads_local, HD)
    key_pos = placed[:, 1].reshape(total, heads_local, HD)
    value_pos = placed[:, 2].reshape(total, heads_local, HD)
    key_valid = (positions < length)[None, None, :]
    prior = prior_logits[0]
    block = min(512, total)
    block_count = total // block

    def block_scores(start):
        query_blk = lax.dynamic_slice_in_dim(query_pos, start, block, 0)
        prior_blk = lax.dynamic_slice_in_dim(prior, start, block, 1).astype(jnp.float32)
        scores = (
            jnp.einsum("qhd,khd->hqk", query_blk, key_pos, preferred_element_type=jnp.float32)
            * scale
            + prior_blk
        )
        return (query_blk, scores)

    def forward_block(block_index, carry):
        raw_buf, context_buf, lse_buf = carry
        start = block_index * block
        query_blk, scores = block_scores(start)
        masked = jnp.where(key_valid, scores, masked_fill)
        largest = jnp.max(masked, axis=-1, keepdims=True)
        exponent = jnp.exp(masked - largest)
        row_total = jnp.sum(exponent, axis=-1, keepdims=True)
        weights = (exponent / row_total).astype(jnp.bfloat16)
        context_blk = jnp.einsum(
            "hqk,khd->qhd", weights, value_pos, preferred_element_type=jnp.float32
        ).astype(jnp.bfloat16)
        raw_buf = lax.dynamic_update_slice_in_dim(raw_buf, scores.astype(jnp.bfloat16), start, 1)
        context_buf = lax.dynamic_update_slice_in_dim(context_buf, context_blk, start, 0)
        lse_buf = lax.dynamic_update_slice_in_dim(lse_buf, largest + jnp.log(row_total), start, 1)
        return (raw_buf, context_buf, lse_buf)

    raw_buf, context_pos, lse_buf = lax.fori_loop(
        0,
        block_count,
        forward_block,
        (
            jnp.zeros((heads_local, total, total), jnp.bfloat16),
            jnp.zeros((total, heads_local, HD), jnp.bfloat16),
            jnp.zeros((heads_local, total, 1), jnp.float32),
        ),
    )
    context_stored = context_pos.reshape(total, local_width)[order_row].reshape(
        total, 1, local_width
    )
    context = lax.all_to_all(
        context_stored, "seq", split_axis=0, concat_axis=1, tiled=True
    ).reshape(local_count, width)
    attended = jnp.dot(context, proj_weight, preferred_element_type=jnp.float32) + proj_bias.astype(
        jnp.float32
    )
    tokens_f = rows.astype(jnp.float32)
    residual_one = tokens_f + attended
    hidden, norm_back_one = jax.vjp(
        layer_norm, residual_one, first_gain.astype(jnp.float32), first_shift.astype(jnp.float32)
    )
    hidden_low = hidden.astype(jnp.bfloat16)
    inner_weight, outer_weight, inner_bias, outer_bias, second_gain, second_shift = (
        lax.all_gather(w_in, "fsdp", axis=0, tiled=True),
        lax.all_gather(w_back, "fsdp", axis=0, tiled=True),
        lax.all_gather(bias_in, "fsdp", axis=0, tiled=True),
        lax.all_gather(bias_back, "fsdp", axis=0, tiled=True),
        lax.all_gather(gain_two, "fsdp", axis=0, tiled=True),
        lax.all_gather(shift_two, "fsdp", axis=0, tiled=True),
    )
    inner = jnp.dot(
        hidden_low, inner_weight, preferred_element_type=jnp.float32
    ) + inner_bias.astype(jnp.float32)
    activated_f, gelu_back = jax.vjp(gelu_exact, inner)
    activated = activated_f.astype(jnp.bfloat16)
    branch = jnp.dot(
        activated, outer_weight, preferred_element_type=jnp.float32
    ) + outer_bias.astype(jnp.float32)
    residual_two = hidden + branch
    normed_two, norm_back_two = jax.vjp(
        layer_norm, residual_two, second_gain.astype(jnp.float32), second_shift.astype(jnp.float32)
    )
    local_order = lax.dynamic_slice_in_dim(order_row, seq_index * local_count, local_count)
    valid_rows = (local_order < length).astype(jnp.float32)[:, None]
    sum_tokens, sum_attended, sum_branch, token_count = lax.psum(
        (
            jnp.sum(valid_rows * tokens_f * tokens_f),
            jnp.sum(valid_rows * attended * attended),
            jnp.sum(valid_rows * branch * branch),
            jnp.sum(valid_rows),
        ),
        ("seq", "fsdp"),
    )
    rms = jnp.sqrt(jnp.stack([sum_tokens, sum_attended, sum_branch]) / (token_count * width))
    d_output = cotangent[0].astype(jnp.float32) * valid_rows
    d_res_two, grad_gain_two, grad_shift_two = norm_back_two(d_output)
    d_branch = d_res_two.astype(jnp.bfloat16)
    grad_bias_back = jnp.sum(d_branch.astype(jnp.float32), axis=0)
    grad_w_back = contract_rows(activated, d_branch)
    d_activated = contract_cols(d_branch, outer_weight)
    d_inner = gelu_back(d_activated)[0].astype(jnp.bfloat16)
    grad_bias_in = jnp.sum(d_inner.astype(jnp.float32), axis=0)
    grad_w_in = contract_rows(hidden_low, d_inner)
    d_hidden = d_res_two + contract_cols(d_inner, inner_weight)
    d_res_one, grad_gain_one, grad_shift_one = norm_back_one(d_hidden)
    d_attended = d_res_one.astype(jnp.bfloat16)
    grad_bias_o = jnp.sum(d_attended.astype(jnp.float32), axis=0)
    grad_w_out = contract_rows(context, d_attended)
    d_context = contract_cols(d_attended, proj_weight).astype(jnp.bfloat16)
    d_context = d_context.reshape(local_count, seq_count, local_width)
    d_context_all = lax.all_to_all(
        d_context, "seq", split_axis=1, concat_axis=0, tiled=True
    ).reshape(total, local_width)
    d_context_pos = d_context_all[inverse].reshape(total, heads_local, HD)

    def backward_block(block_index, carry):
        dprior_buf, dquery_buf, dkey_acc, dvalue_acc = carry
        start = block_index * block
        query_blk, scores = block_scores(start)
        masked = jnp.where(key_valid, scores, masked_fill)
        lse_blk = lax.dynamic_slice_in_dim(lse_buf, start, block, 1)
        probability = jnp.exp(masked - lse_blk)
        weights = probability.astype(jnp.bfloat16)
        dcontext_blk = lax.dynamic_slice_in_dim(d_context_pos, start, block, 0)
        d_prob = jnp.einsum(
            "qhd,khd->hqk", dcontext_blk, value_pos, preferred_element_type=jnp.float32
        )
        row_term = jnp.sum(probability * d_prob, axis=-1, keepdims=True)
        d_scores = (probability * (d_prob - row_term)).astype(jnp.bfloat16)
        dprior_buf = lax.dynamic_update_slice_in_dim(dprior_buf, d_scores, start, 1)
        dquery_blk = (
            jnp.einsum("hqk,khd->qhd", d_scores, key_pos, preferred_element_type=jnp.float32)
            * scale
        )
        dquery_buf = lax.dynamic_update_slice_in_dim(dquery_buf, dquery_blk, start, 0)
        dkey_acc = (
            dkey_acc
            + jnp.einsum("hqk,qhd->khd", d_scores, query_blk, preferred_element_type=jnp.float32)
            * scale
        )
        dvalue_acc = dvalue_acc + jnp.einsum(
            "hqk,qhd->khd", weights, dcontext_blk, preferred_element_type=jnp.float32
        )
        return (dprior_buf, dquery_buf, dkey_acc, dvalue_acc)

    dprior_buf, dquery_buf, dkey_acc, dvalue_acc = lax.fori_loop(
        0,
        block_count,
        backward_block,
        (
            jnp.zeros((heads_local, total, total), jnp.bfloat16),
            jnp.zeros((total, heads_local, HD), jnp.float32),
            jnp.zeros((total, heads_local, HD), jnp.float32),
            jnp.zeros((total, heads_local, HD), jnp.float32),
        ),
    )
    d_joint_pos = jnp.stack(
        [
            dquery_buf.reshape(total, local_width),
            dkey_acc.reshape(total, local_width),
            dvalue_acc.reshape(total, local_width),
        ],
        axis=1,
    ).astype(jnp.bfloat16)
    d_joint_stored = d_joint_pos[order_row].reshape(total, 3, 1, local_width)
    d_joint = lax.all_to_all(
        d_joint_stored, "seq", split_axis=0, concat_axis=2, tiled=True
    ).reshape(local_count, 3 * width)
    grad_bias_q = jnp.sum(d_joint[:, :width].astype(jnp.float32), axis=0)
    grad_bias_v = jnp.sum(d_joint[:, 2 * width :].astype(jnp.float32), axis=0)
    grad_w_qkv = contract_rows(rows, d_joint)
    tokens_grad = (d_res_one + contract_cols(d_joint, qkv_weight)).astype(jnp.bfloat16)
    (
        pair_qkv,
        pair_out,
        pair_in,
        pair_back,
        pair_bias_q,
        pair_bias_v,
        pair_bias_o,
        pair_gain_one,
        pair_shift_one,
        pair_bias_in,
        pair_bias_back,
        pair_gain_two,
        pair_shift_two,
    ) = (
        lax.psum(grad_w_qkv.astype(jnp.bfloat16), "seq").astype(jnp.float32),
        lax.psum(grad_w_out.astype(jnp.bfloat16), "seq").astype(jnp.float32),
        lax.psum(grad_w_in.astype(jnp.bfloat16), "seq").astype(jnp.float32),
        lax.psum(grad_w_back.astype(jnp.bfloat16), "seq").astype(jnp.float32),
        lax.psum(grad_bias_q.astype(jnp.bfloat16), "seq").astype(jnp.float32),
        lax.psum(grad_bias_v.astype(jnp.bfloat16), "seq").astype(jnp.float32),
        lax.psum(grad_bias_o.astype(jnp.bfloat16), "seq").astype(jnp.float32),
        lax.psum(grad_gain_one.astype(jnp.bfloat16), "seq").astype(jnp.float32),
        lax.psum(grad_shift_one.astype(jnp.bfloat16), "seq").astype(jnp.float32),
        lax.psum(grad_bias_in.astype(jnp.bfloat16), "seq").astype(jnp.float32),
        lax.psum(grad_bias_back.astype(jnp.bfloat16), "seq").astype(jnp.float32),
        lax.psum(grad_gain_two.astype(jnp.bfloat16), "seq").astype(jnp.float32),
        lax.psum(grad_shift_two.astype(jnp.bfloat16), "seq").astype(jnp.float32),
    )
    owned = (
        lax.psum_scatter(pair_qkv, "fsdp", scatter_dimension=0, tiled=True),
        lax.psum_scatter(pair_out, "fsdp", scatter_dimension=0, tiled=True),
        lax.psum_scatter(pair_in, "fsdp", scatter_dimension=0, tiled=True),
        lax.psum_scatter(pair_back, "fsdp", scatter_dimension=0, tiled=True),
        lax.psum_scatter(pair_bias_q, "fsdp", scatter_dimension=0, tiled=True),
        lax.psum_scatter(pair_bias_v, "fsdp", scatter_dimension=0, tiled=True),
        lax.psum_scatter(pair_bias_o, "fsdp", scatter_dimension=0, tiled=True),
        lax.psum_scatter(pair_gain_one, "fsdp", scatter_dimension=0, tiled=True),
        lax.psum_scatter(pair_shift_one, "fsdp", scatter_dimension=0, tiled=True),
        lax.psum_scatter(pair_bias_in, "fsdp", scatter_dimension=0, tiled=True),
        lax.psum_scatter(pair_bias_back, "fsdp", scatter_dimension=0, tiled=True),
        lax.psum_scatter(pair_gain_two, "fsdp", scatter_dimension=0, tiled=True),
        lax.psum_scatter(pair_shift_two, "fsdp", scatter_dimension=0, tiled=True),
    )
    return (
        normed_two.astype(jnp.bfloat16)[None],
        raw_buf[None],
        tokens_grad[None],
        dprior_buf[None],
        owned[0],
        owned[1],
        owned[2],
        owned[3],
        owned[4],
        owned[5],
        owned[6],
        owned[7],
        owned[8],
        owned[9],
        owned[10],
        owned[11],
        owned[12],
        rms,
    )


def solution(mesh):
    return jax.shard_map(
        body,
        mesh=mesh,
        in_specs=(
            P("fsdp", "seq", None),
            P("fsdp", "seq", None, None),
            P("fsdp"),
            P("fsdp", None),
            P("fsdp", "seq", None),
            P("fsdp", None),
            P("fsdp", None),
            P("fsdp", None),
            P("fsdp", None),
            P("fsdp"),
            P("fsdp"),
            P("fsdp"),
            P("fsdp"),
            P("fsdp"),
            P("fsdp"),
            P("fsdp"),
            P("fsdp"),
            P("fsdp"),
        ),
        out_specs=(
            P("fsdp", "seq", None),
            P("fsdp", "seq", None, None),
            P("fsdp", "seq", None),
            P("fsdp", "seq", None, None),
            P("fsdp", None),
            P("fsdp", None),
            P("fsdp", None),
            P("fsdp", None),
            P("fsdp"),
            P("fsdp"),
            P("fsdp"),
            P("fsdp"),
            P("fsdp"),
            P("fsdp"),
            P("fsdp"),
            P("fsdp"),
            P("fsdp"),
            P(),
        ),
        check_vma=False,
    )
```

profile of v0, /device:TPU:0, one launch (start us, length us, event | category | flops | bytes accessed | tf_op | source)
XLA Modules:
  0.0 1158.4 jit_solution(11270746098248359767)
XLA Ops:
  19.6 63.9 %all-reduce.20 = (bf16[768]{0:T(1024)(128)(2,1)S(1)}, bf16[768]{0:T(1024)(128)(2,1)S(1)}, bf16[768]{0:T(1024)(128)(2,1)}, bf16[768]{0:T(1024)(128)(2,1)}, bf16[7...) all-reduce(bf16[768]{0:T(1024)(128)(2,1)S(1)} %dynamic-update-slice, ...), channel_id=1, replica_groups=mesh['seq'=2,'fsdp'=16] {'fsdp'}, use_global_device_ids=true, to_apply=%add.1 | all-reduce | flops 9216 | bytes 36864
  105.4 17.6 %all-to-all-done = bf16[512,3,2,384]{3,0,1,2:T(8,128)(2,1)S(1)} async-done(((bf16[512,3,2,384]{3,0,1,2:T(8,128)(2,1)}), bf16[512,3,2,384]{3,0,1,2:T(8,128)(2,1)S(1)}, u32[]{:S(2)}, u32[]{:S(2)}) %all-to-all-start) | async-done | bytes 2359328 | tf_op jit(solution)/shard_map/all_to_all | solution.py:84
  155.7 31.1 %while.38 = (s32[]{:T(128)}, bf16[6,1024,1024]{2,1,0:T(8,128)(2,1)}, bf16[1024,6,64]{0,2,1:T(8,128)(2,1)S(1)}, f32[6,1024,1]{1,0,2:T(8,128)S(1)}, bf16[1024,6,64...) while((s32[]{:T(128)}, ...), condition=%wide.region_4.5_spmd.clone, body=%wide.region_1.4_spmd.clone.sunk | while | flops 846395392 | bytes 65397944 | solution.py:127
  156.4 7.3 convert_dynamic-update-slice_fusion.2
  171.9 7.4 convert_dynamic-update-slice_fusion.2
  216.4 19.9 %multiply_convert_fusion.1 = (bf16[512,3072]{1,0:T(8,128)(2,1)}, f32[512,3072]{1,0:T(8,128)}, f32[512,3072]{1,0:T(8,128)}) fusion(f32[3072]{0:T(1024)S(1)} %convert_element_type.217, bf16[768,3072]{1,0:T(8,128)(2,1)} %all-gather.9.cloned.1.call-done, f32[512,768]{1,0:T(8,128)S(1)} %get-tuple-element.679, f32[768]{0:T(1024)S(1)} %convert_element_type.215, ...), kind=kOutput, calls=%fused_computation.47 | convolution fusion | flops 2521694208 | bytes 22042624 | tf_op jit(solution)/shard_map/dot_general | solution.py:160
  247.7 8.6 fusion.61
  267.0 7.9 all-to-all-done.2
  289.8 65.8 %while.39 = (s32[]{:T(128)}, bf16[6,1024,1024]{2,1,0:T(8,128)(2,1)}, bf16[1024,6,64]{0,2,1:T(8,128)(2,1)}, f32[1024,6,64]{0,2,1:T(8,128)S(1)}, f32[1024,6,64]{0,...) while((s32[]{:T(128)}, ...), condition=%wide.region_15.16_spmd.clone, body=%wide.region_13.0_spmd.clone.sunk | while | flops 2050029568 | bytes 127470920 | solution.py:235
  293.6 9.4 multiply_reduce_fusion.6
  310.0 8.9 constant_dynamic-update-slice_fusion.2
  326.3 9.5 multiply_reduce_fusion.6
  335.8 7.4 bitcast_add_fusion.5
  343.2 8.9 constant_dynamic-update-slice_fusion.2
  373.0 10.2 gather_fusion.3
  402.5 13.4 %all-to-all-done.3 = bf16[1024,3,1,384]{3,1,2,0:T(4,128)(2,1)S(1)} async-done(((bf16[1024,3,1,384]{3,1,2,0:T(4,128)(2,1)}), bf16[1024,3,1,384]{3,1,2,0:T(4,128)(2,1)S(1)}, u32[]{:S(2)}, u32[]{:S(2)}) %all-to-all-start.3) | async-done | bytes 2359328 | tf_op jit(solution)/shard_map/all_to_all | solution.py:255
  424.3 334.0 %all-reduce.25.cloned.1.call-done = (bf16[768,2304]{0,1:T(8,128)(2,1)}, bf16[768,768]{1,0:T(8,128)(2,1)}, bf16[768,3072]{1,0:T(8,128)(2,1)}, bf16[3072,768]{1,0:T(8,128)(2,1)}) async-done(((bf16[768,2304]{0,1:T(8,128)(2,1)}, bf16[768,768]{1,0:T(8,128)(2,1)}, bf16[768,3072]{1,0:T(8,128)(2,1)}, bf16[3072,768]{1,0:T(8,128)(2,1)}), (bf16[768,2304]{0,1:T(8,128)(2,1)}, bf16[768,768]{1,0:T(8,128)(2,1)}, ...) | async-done | bytes 14155792 | tf_op jit(solution)/shard_map/psum | solution.py:277
  767.3 7.3 convert_element_type.238
  782.9 40.3 %all-reduce.18 = (f32[1]{0:T(128)}, f32[1]{0:T(128)}, f32[1]{0:T(128)}, f32[]{:T(128)}) all-reduce(f32[1]{0:T(128)} %bitcast.38, f32[1]{0:T(128)} %bitcast.37, f32[1]{0:T(128)} %bitcast.36, f32[]{:T(128)} %get-tuple-element.662), channel_id=1, replica_groups=mesh['seq'=2,'fsdp'=16] {'seq','fsdp'}, use_global_device_ids=true, to_apply=%region_56.57 | all-reduce | flops 4 | bytes 32 | tf_op jit(solution)/shard_map/psum | solution.py:174
  826.7 9.1 all-reduce.21
  835.8 59.7 %all-reduce.19 = (f32[768]{0:T(1024)S(1)}, f32[768]{0:T(1024)S(1)}, f32[768]{0:T(1024)S(1)}, f32[768]{0:T(1024)S(1)}, f32[768]{0:T(1024)S(1)}, /*index=5*/f32[30...) all-reduce(bf16[768]{0:T(1024)(128)(2,1)S(1)} %get-tuple-element.64, ...), channel_id=6, replica_groups=mesh['seq'=2,'fsdp'=16] {'fsdp'}, use_global_device_ids=true, to_apply=%region_26.27.clone | all-reduce | flops 9216 | bytes 55296
  906.5 13.9 %reduce-scatter.13.cloned.1.call-done = f32[48,2304]{1,0:T(8,128)} async-done(((f32[768,2304]{1,0:T(8,128)}), f32[48,2304]{1,0:T(8,128)}) %reduce-scatter.13.cloned.1.call-update) | async-done | bytes 442384
  920.4 115.6 %reduce-scatter.9.cloned.1.call-done = f32[48,3072]{1,0:T(8,128)} async-done(((f32[768,3072]{1,0:T(8,128)}), f32[48,3072]{1,0:T(8,128)}) %reduce-scatter.9.cloned.1.call-update) | async-done | bytes 589840 | tf_op jit(solution)/shard_map/reduce_scatter | solution.py:294
  1036.0 115.5 %reduce-scatter.11.cloned.1.call-done = f32[192,768]{1,0:T(8,128)} async-done(((f32[3072,768]{1,0:T(8,128)}), f32[192,768]{1,0:T(8,128)}) %reduce-scatter.11.cloned.1.call-update) | async-done | bytes 589840 | tf_op jit(solution)/shard_map/reduce_scatter | solution.py:295
  (273 shorter events, 243.4 us)
Async XLA Ops:
  7.2 76.4 %all-gather.5.cloned.1.call-start = ((), (), s32[]{:S(2)}) async-start(), calls=%async_computation.8 | async-start | bytes 3760128 | tf_op jit(solution)/shard_map/all_gather | solution.py:58
  7.9 204.6 %all-gather.7.cloned.1.call-start = ((), (), s32[]{:S(2)}) async-start(), calls=%async_computation.9 | async-start | bytes 1253376 | tf_op jit(solution)/shard_map/all_gather | solution.py:59
  8.7 207.7 %all-gather.9.cloned.1.call-start = ((), (), s32[]{:S(2)}) async-start(), calls=%async_computation.10 | async-start | bytes 5013504 | tf_op jit(solution)/shard_map/all_gather | solution.py:153
  95.7 27.3 %all-to-all-start = ((bf16[512,3,2,384]{3,0,1,2:T(8,128)(2,1)}), bf16[512,3,2,384]{3,0,1,2:T(8,128)(2,1)S(1)}, u32[]{:S(2)}, u32[]{:S(2)}) async-start(bf16[512,3,2,384]{3,0,1,2:T(8,128)(2,1)} %copy.86), calls=%async_computation | async-start | bytes 4718592 | tf_op jit(solution)/shard_map/all_to_all | solution.py:84
  99.6 136.6 %all-gather.11.cloned.1.call-start = ((), (), s32[]{:S(2)}) async-start(), calls=%async_computation.11 | async-start | bytes 5013504 | tf_op jit(solution)/shard_map/all_gather | solution.py:154
  194.7 12.8 %all-to-all-start.1 = ((bf16[2,2,98304]{2,1,0:T(2,128)(2,1)}), bf16[2,2,98304]{2,1,0:T(2,128)(2,1)}, u32[]{:S(2)}, u32[]{:S(2)}) async-start(bf16[2,2,98304]{2,1,0:T(2,128)(2,1)} %reshape.336), calls=%async_computation.1 | async-start | bytes 1572864 | tf_op jit(solution)/shard_map/all_to_all | solution.py:140
  200.2 59.8 %copy-start.23 = (f32[768]{0:T(1024)}, f32[768]{0:T(1024)S(1)}, u32[]{:S(2)}) copy-start(f32[768]{0:T(1024)S(1)} %convert_element_type.214) | copy-start | bytes 9220
  216.0 44.0 %copy-start.4 = (f32[512,768]{1,0:T(8,128)}, f32[512,768]{1,0:T(8,128)S(1)}, u32[]{:S(2)}) copy-start(f32[512,768]{1,0:T(8,128)S(1)} %get-tuple-element.679) | copy-start | bytes 4718596
  216.0 44.0 %copy-start.21 = (f32[512]{0:T(512)}, f32[512]{0:T(512)S(1)}, u32[]{:S(2)}) copy-start(f32[512]{0:T(512)S(1)} %broadcast_multiply_fusion.1) | copy-start | bytes 6148
  263.5 11.5 all-to-all-start.2
  383.2 32.6 %all-to-all-start.3 = ((bf16[1024,3,1,384]{3,1,2,0:T(4,128)(2,1)}), bf16[1024,3,1,384]{3,1,2,0:T(4,128)(2,1)S(1)}, u32[]{:S(2)}, u32[]{:S(2)}) async-start(bf16[1024,3,1,384]{3,1,2,0:T(4,128)(2,1)} %bitcast.149), calls=%async_computation.3 | async-start | bytes 6291456 | tf_op jit(solution)/shard_map/all_to_all | solution.py:255
  387.2 371.1 %all-reduce.25.cloned.1.call-start = ((), (), s32[]{:S(2)}) async-start(), calls=%async_computation.16 | async-start | bytes 28311552 | tf_op jit(solution)/shard_map/psum | solution.py:277
  424.3 482.2 %reduce-scatter.7.cloned.1.call-start = ((), (), s32[]{:S(2)}) async-start(), calls=%async_computation.12 | async-start | bytes 2506752 | tf_op jit(solution)/shard_map/reduce_scatter | solution.py:293
  761.2 159.2 %reduce-scatter.13.cloned.1.call-start = ((), (), s32[]{:S(2)}) async-start(), calls=%async_computation.15 | async-start | bytes 7520256
  767.2 268.8 %reduce-scatter.9.cloned.1.call-start = ((), (), s32[]{:S(2)}) async-start(), calls=%async_computation.13 | async-start | bytes 10027008 | tf_op jit(solution)/shard_map/reduce_scatter | solution.py:294
  774.6 377.0 %reduce-scatter.11.cloned.1.call-start = ((), (), s32[]{:S(2)}) async-start(), calls=%async_computation.14 | async-start | bytes 10027008 | tf_op jit(solution)/shard_map/reduce_scatter | solution.py:295
  781.5 45.1 %copy-start.31 = (bf16[768]{0:T(1024)(128)(2,1)S(1)}, bf16[768]{0:T(1024)(128)(2,1)}, u32[]{:S(2)}) copy-start(bf16[768]{0:T(1024)(128)(2,1)} %get-tuple-element.580) | copy-start | bytes 4612
  781.6 45.1 %copy-start.32 = (bf16[768]{0:T(1024)(128)(2,1)S(1)}, bf16[768]{0:T(1024)(128)(2,1)}, u32[]{:S(2)}) copy-start(bf16[768]{0:T(1024)(128)(2,1)} %get-tuple-element.582) | copy-start | bytes 4612
  781.6 45.1 %copy-start.33 = (bf16[768]{0:T(1024)(128)(2,1)S(1)}, bf16[768]{0:T(1024)(128)(2,1)}, u32[]{:S(2)}) copy-start(bf16[768]{0:T(1024)(128)(2,1)} %get-tuple-element.664) | copy-start | bytes 4612
  781.6 45.1 %copy-start.34 = (bf16[768]{0:T(1024)(128)(2,1)S(1)}, bf16[768]{0:T(1024)(128)(2,1)}, u32[]{:S(2)}) copy-start(bf16[768]{0:T(1024)(128)(2,1)} %get-tuple-element.668) | copy-start | bytes 4612
  781.6 45.1 %copy-start.35 = (bf16[3072]{0:T(1024)(128)(2,1)S(1)}, bf16[3072]{0:T(1024)(128)(2,1)}, u32[]{:S(2)}) copy-start(bf16[3072]{0:T(1024)(128)(2,1)} %get-tuple-element.666) | copy-start | bytes 18436
  781.6 45.1 %copy-start.45 = (bf16[768]{0:T(1024)(128)(2,1)S(1)}, bf16[768]{0:T(1024)(128)(2,1)}, u32[]{:S(2)}) copy-start(bf16[768]{0:T(1024)(128)(2,1)} %get-tuple-element.569) | copy-start | bytes 4612
  781.6 45.1 %copy-start.46 = (bf16[768]{0:T(1024)(128)(2,1)S(1)}, bf16[768]{0:T(1024)(128)(2,1)}, u32[]{:S(2)}) copy-start(bf16[768]{0:T(1024)(128)(2,1)} %get-tuple-element.575) | copy-start | bytes 4612
  781.6 119.2 %copy-start.28 = (f32[512]{0:T(512)S(1)}, f32[512]{0:T(512)}, u32[]{:S(2)}) copy-start(f32[512]{0:T(512)} %copy-done.27) | copy-start | bytes 6148
  (45 other events, 403.9 us)
Sparse Core Ops, SparseCore 0:
  10.3 50.2 all-gather.4
  62.8 36.8 all-gather.6
  102.0 51.9 all-gather.8
  156.1 51.7 all-gather.10
  424.4 333.8 all-reduce.24
  762.5 63.8 reduce-scatter.6
  831.0 89.3 reduce-scatter.12
  925.1 110.9 reduce-scatter.8
  1040.7 110.8 reduce-scatter.10
where the time goes:
time: 1170 us; the launch traced here: 1160 us
  waiting for transfers between devices  627 us (54%)
  blocking collectives  173 us (15%)
  matrix products  142 us (12%)
  local copies, waits for them, and re-layouts  115 us (10%)
  other arithmetic  66 us (6%)
  between operations  19 us (2%)
  starting transfers between devices  16.5 us (1%)
    psum x1, waiting for transfers between devices, body(): lax.psum(grad_w_qkv.astype(jnp.bfloat16), 'seq').astype(jnp.float32)  334 us
    unnamed x2, blocking collectives  124 us
    reduce_scatter x1, waiting for transfers between devices, body(): lax.psum_scatter(pair_in, 'fsdp', scatter_dimension=0, tiled=True)  116 us
    reduce_scatter x1, waiting for transfers between devices, body(): lax.psum_scatter(pair_back, 'fsdp', scatter_dimension=0, tiled=True)  116 us
    psum x1, blocking collectives, body(): lax.psum((jnp.sum(valid_rows * tokens_f * tokens_f), jnp.sum(valid_rows *...  40.3 us
    dot_general x4, matrix products, block_scores(): jnp.einsum('qhd,khd->hqk', query_blk, key_pos, preferred_element_type=jnp...  33.6 us
    unnamed x132, local copies, waits for them, and re-layouts  24.9 us
  transfers between devices with their start and end apart: 13, of which 8 were waited for; matrix products, arithmetic and copies ran while one was open for 15% of the time, Pallas kernels for 0%

commit v1 on v0

--- a/solution.py
+++ b/solution.py
@@ -274,7 +274,7 @@
         pair_gain_two,
         pair_shift_two,
     ) = (
-        lax.psum(grad_w_qkv.astype(jnp.bfloat16), "seq").astype(jnp.float32),
+        jnp.sum(lax.all_gather(grad_w_qkv.astype(jnp.bfloat16), "seq"), axis=0).astype(jnp.float32),
         lax.psum(grad_w_out.astype(jnp.bfloat16), "seq").astype(jnp.float32),
         lax.psum(grad_w_in.astype(jnp.bfloat16), "seq").astype(jnp.float32),
         lax.psum(grad_w_back.astype(jnp.bfloat16), "seq").astype(jnp.float32),

time: 1170 us -> 1080 us (0.923)
  waiting for transfers between devices: 627 us -> 399 us
  other arithmetic: 66 us -> 144 us
  blocking collectives: 173 us -> 222 us
  local copies, waits for them, and re-layouts: 115 us -> 131 us
    psum x1, waiting for transfers between devices: 334 us -> 103 us  [body(): lax.psum(grad_w_out.astype(jnp.bfloat16), 'seq').astype(jnp.float32)]
    all_gather x0 -> x1, waiting for transfers between devices: none -> 87.7 us  [body(): lax.all_gather(grad_w_qkv.astype(jnp.bfloat16), 'seq')]
    reduce_sum x0 -> x1, other arithmetic: none -> 74.5 us  [body(): jnp.sum(lax.all_gather(grad_w_qkv.astype(jnp.bfloat16), 'seq'), axis=0)]
    reduce_scatter x1, waiting for transfers between devices: 116 us -> 65.6 us  [body(): lax.psum_scatter(pair_in, 'fsdp', scatter_dimension=0, tiled=True)]
    all_to_all x0 -> x1, blocking collectives: none -> 48.9 us  [body(): lax.all_to_all(d_joint_stored, 'seq', split_axis=0, concat_axis=2, tiled=...]
    all_gather x0 -> x1, local copies, waits for them, and re-layouts: none -> 15.2 us  [body(): lax.all_gather(grad_w_qkv.astype(jnp.bfloat16), 'seq')]
    unnamed x10 -> x11, waiting for transfers between devices: 16.6 us -> 2.68 us
    all_to_all x1 -> x0, waiting for transfers between devices: 13.4 us -> none  [body(): lax.all_to_all(d_joint_stored, 'seq', split_axis=0, concat_axis=2, tiled=...]
  transfers between devices with their start and end apart: 13 -> 13, of which waited for: 8 -> 6; matrix products, arithmetic and copies ran while one was open for 15% -> 36% of each run, Pallas kernels for 0% -> 0%
where the time goes in v1:
time: 1080 us; the launch traced here: 1070 us
  waiting for transfers between devices  399 us (37%)
  blocking collectives  222 us (21%)
  matrix products  147 us (14%)
  other arithmetic  144 us (13%)
  local copies, waits for them, and re-layouts  131 us (12%)
  between operations  19.4 us (2%)
  starting transfers between devices  12.9 us (1%)
    unnamed x2, blocking collectives  122 us
    reduce_scatter x1, waiting for transfers between devices, body(): lax.psum_scatter(pair_back, 'fsdp', scatter_dimension=0, tiled=True)  115 us
    psum x1, waiting for transfers between devices, body(): lax.psum(grad_w_out.astype(jnp.bfloat16), 'seq').astype(jnp.float32)  103 us
    all_gather x1, waiting for transfers between devices, body(): lax.all_gather(grad_w_qkv.astype(jnp.bfloat16), 'seq')  87.7 us
    reduce_sum x1, other arithmetic, body(): jnp.sum(lax.all_gather(grad_w_qkv.astype(jnp.bfloat16), 'seq'), axis=0)  74.5 us
    reduce_scatter x1, waiting for transfers between devices, body(): lax.psum_scatter(pair_in, 'fsdp', scatter_dimension=0, tiled=True)  65.6 us
    all_to_all x1, blocking collectives, body(): lax.all_to_all(d_joint_stored, 'seq', split_axis=0, concat_axis=2, tiled=...  48.9 us
    psum x1, blocking collectives, body(): lax.psum((jnp.sum(valid_rows * tokens_f * tokens_f), jnp.sum(valid_rows *...  41.7 us
  transfers between devices with their start and end apart: 13, of which 6 were waited for; matrix products, arithmetic and copies ran while one was open for 36% of the time, Pallas kernels for 0%

profile of v1, /device:TPU:0, one launch (start us, length us, event | category | flops | bytes accessed | tf_op | source)
XLA Modules:
  0.0 1074.9 jit_solution(13788863984707627514)
XLA Ops:
  19.6 63.9 %all-reduce.20 = (bf16[768]{0:T(1024)(128)(2,1)S(1)}, bf16[768]{0:T(1024)(128)(2,1)S(1)}, bf16[768]{0:T(1024)(128)(2,1)}, bf16[768]{0:T(1024)(128)(2,1)}, bf16[7...) all-reduce(bf16[768]{0:T(1024)(128)(2,1)S(1)} %dynamic-update-slice, ...), channel_id=1, replica_groups=mesh['seq'=2,'fsdp'=16] {'fsdp'}, use_global_device_ids=true, to_apply=%add.1 | all-reduce | flops 9216 | bytes 36864
  105.5 17.5 %all-to-all-done = bf16[512,3,2,384]{3,0,1,2:T(8,128)(2,1)S(1)} async-done(((bf16[512,3,2,384]{3,0,1,2:T(8,128)(2,1)}), bf16[512,3,2,384]{3,0,1,2:T(8,128)(2,1)S(1)}, u32[]{:S(2)}, u32[]{:S(2)}) %all-to-all-start) | async-done | bytes 2359328 | tf_op jit(solution)/shard_map/all_to_all | solution.py:84
  155.7 31.1 %while.38 = (s32[]{:T(128)}, bf16[6,1024,1024]{2,1,0:T(8,128)(2,1)}, bf16[1024,6,64]{0,2,1:T(8,128)(2,1)S(1)}, f32[6,1024,1]{1,0,2:T(8,128)S(1)}, bf16[1024,6,64...) while((s32[]{:T(128)}, ...), condition=%wide.region_4.5_spmd.clone, body=%wide.region_1.4_spmd.clone.sunk | while | flops 846395392 | bytes 65397944 | solution.py:127
  219.9 20.9 %multiply_convert_fusion.1 = (bf16[512,3072]{1,0:T(8,128)(2,1)}, f32[512,3072]{1,0:T(8,128)}, f32[512,3072]{1,0:T(8,128)}) fusion(f32[3072]{0:T(1024)S(1)} %convert_element_type.219, bf16[768,3072]{1,0:T(8,128)(2,1)} %all-gather.11.cloned.1.call-done, f32[512,768]{1,0:T(8,128)} %copy-done.4, f32[768]{0:T(1024)S(1)} %convert_element_type.217, ...), kind=kOutput, calls=%fused_computation.47 | convolution fusion | flops 2521694208 | bytes 22042624 | tf_op jit(solution)/shard_map/dot_general | solution.py:160
  252.8 10.0 fusion.61
  304.6 66.7 %while.39 = (s32[]{:T(128)}, bf16[6,1024,1024]{2,1,0:T(8,128)(2,1)}, bf16[1024,6,64]{0,2,1:T(8,128)(2,1)}, f32[1024,6,64]{0,2,1:T(8,128)S(1)}, f32[1024,6,64]{0,...) while((s32[]{:T(128)}, ...), condition=%wide.region_15.16_spmd.clone, body=%wide.region_13.0_spmd.clone.sunk | while | flops 2050029568 | bytes 127470920 | solution.py:235
  308.4 9.4 multiply_reduce_fusion.6
  317.8 7.4 bitcast_add_fusion.5
  325.3 9.1 constant_dynamic-update-slice_fusion.2
  341.9 9.5 multiply_reduce_fusion.6
  351.4 7.4 bitcast_add_fusion.5
  358.8 9.0 constant_dynamic-update-slice_fusion.2
  386.0 8.3 pad_maximum_fusion
  400.8 48.9 %all_to_all.60 = bf16[1024,3,1,384]{3,1,2,0:T(4,128)(2,1)S(1)} all-to-all(bf16[1024,3,1,384]{3,1,2,0:T(4,128)(2,1)S(1)} %bitcast.151), channel_id=1, replica_groups=mesh['seq'=2,'fsdp'=16] {'seq'}, dimensions={0} | all-to-all | bytes 4718592 | tf_op jit(solution)/shard_map/all_to_all | solution.py:255
  458.0 103.3 %all-reduce.25.cloned.1.call-done = (bf16[768,768]{1,0:T(8,128)(2,1)}, bf16[768,3072]{1,0:T(8,128)(2,1)}, bf16[3072,768]{1,0:T(8,128)(2,1)}) async-done(((bf16[768,768]{1,0:T(8,128)(2,1)}, bf16[768,3072]{1,0:T(8,128)(2,1)}, bf16[3072,768]{1,0:T(8,128)(2,1)}), (bf16[768,768]{1,0:T(8,128)(2,1)}, bf16[768,3072]{1,0:T(8,128)(2,1)}, bf16[3072,768]{1,0:T(8,128)(2,1)})) %all-reduce.25.cloned.1.call-update) | async-done | bytes 10616848 | tf_op jit(solution)/shard_map/psum | solution.py:278
  564.2 87.7 %all-gather.15.cloned.1.call-done = bf16[1536,2304]{0,1:T(8,128)(2,1)} async-done(((bf16[768,2304]{0,1:T(8,128)(2,1)}), bf16[1536,2304]{0,1:T(8,128)(2,1)}) %all-gather.15.cloned.1.call-update) | async-done | bytes 7077904 | tf_op jit(solution)/shard_map/all_gather | solution.py:277
  651.9 15.2 %reshape.274 = bf16[2,768,2304]{1,0,2:T(2,128)(2,1)} reshape(bf16[1536,2304]{0,1:T(8,128)(2,1)} %all-gather.15.cloned.1.call-done) | data formatting | bytes 14155776 | tf_op jit(solution)/shard_map/all_gather | solution.py:277
  667.1 74.5 %reduce_sum.282 = bf16[768,2304]{0,1:T(8,128)(2,1)S(1)} reduce(bf16[2,768,2304]{1,0,2:T(2,128)(2,1)} %reshape.274, bf16[]{:T(256)} %constant.166.clone.1), dimensions={0}, to_apply=%region_16.17 | reduce | flops 1769472 | bytes 10616834 | tf_op jit(solution)/shard_map/reduce_sum | solution.py:277
  754.1 7.5 convert_element_type.242
  763.3 41.7 %all-reduce.18 = (f32[1]{0:T(128)}, f32[1]{0:T(128)}, f32[1]{0:T(128)}, f32[]{:T(128)}) all-reduce(f32[1]{0:T(128)} %bitcast.38, f32[1]{0:T(128)} %bitcast.37, f32[1]{0:T(128)} %bitcast.36, f32[]{:T(128)} %get-tuple-element.625), channel_id=1, replica_groups=mesh['seq'=2,'fsdp'=16] {'seq','fsdp'}, use_global_device_ids=true, to_apply=%region_56.57 | all-reduce | flops 4 | bytes 32 | tf_op jit(solution)/shard_map/psum | solution.py:174
  808.5 9.1 all-reduce.21
  817.7 58.5 %all-reduce.19 = (f32[768]{0:T(1024)S(1)}, f32[768]{0:T(1024)S(1)}, f32[768]{0:T(1024)S(1)}, f32[768]{0:T(1024)S(1)}, f32[768]{0:T(1024)S(1)}, /*index=5*/f32[30...) all-reduce(bf16[768]{0:T(1024)(128)(2,1)S(1)} %get-tuple-element.61, ...), channel_id=7, replica_groups=mesh['seq'=2,'fsdp'=16] {'fsdp'}, use_global_device_ids=true, to_apply=%region_26.27.clone | all-reduce | flops 9216 | bytes 55296
  886.9 65.6 %reduce-scatter.9.cloned.1.call-done = f32[48,3072]{1,0:T(8,128)} async-done(((f32[768,3072]{1,0:T(8,128)}), f32[48,3072]{1,0:T(8,128)}) %reduce-scatter.9.cloned.1.call-update) | async-done | bytes 589840 | tf_op jit(solution)/shard_map/reduce_scatter | solution.py:294
  952.5 115.4 %reduce-scatter.11.cloned.1.call-done = f32[192,768]{1,0:T(8,128)} async-done(((f32[3072,768]{1,0:T(8,128)}), f32[192,768]{1,0:T(8,128)}) %reduce-scatter.11.cloned.1.call-update) | async-done | bytes 589840 | tf_op jit(solution)/shard_map/reduce_scatter | solution.py:295
  (265 shorter events, 255.4 us)
Async XLA Ops:
  7.2 76.4 %all-gather.7.cloned.1.call-start = ((), (), s32[]{:S(2)}) async-start(), calls=%async_computation.8 | async-start | bytes 3760128 | tf_op jit(solution)/shard_map/all_gather | solution.py:58
  7.9 207.0 %all-gather.9.cloned.1.call-start = ((), (), s32[]{:S(2)}) async-start(), calls=%async_computation.9 | async-start | bytes 1253376 | tf_op jit(solution)/shard_map/all_gather | solution.py:59
  8.7 211.3 %all-gather.11.cloned.1.call-start = ((), (), s32[]{:S(2)}) async-start(), calls=%async_computation.10 | async-start | bytes 5013504 | tf_op jit(solution)/shard_map/all_gather | solution.py:153
  95.7 27.3 %all-to-all-start = ((bf16[512,3,2,384]{3,0,1,2:T(8,128)(2,1)}), bf16[512,3,2,384]{3,0,1,2:T(8,128)(2,1)S(1)}, u32[]{:S(2)}, u32[]{:S(2)}) async-start(bf16[512,3,2,384]{3,0,1,2:T(8,128)(2,1)} %copy.101), calls=%async_computation | async-start | bytes 4718592 | tf_op jit(solution)/shard_map/all_to_all | solution.py:84
  99.6 141.2 %all-gather.13.cloned.1.call-start = ((), (), s32[]{:S(2)}) async-start(), calls=%async_computation.11 | async-start | bytes 5013504 | tf_op jit(solution)/shard_map/all_gather | solution.py:154
  105.5 21.5 %copy-start.22 = (s32[1024]{0:T(1024)}, s32[1024]{0:T(1024)S(1)}, u32[]{:S(2)}) copy-start(s32[1024]{0:T(1024)S(1)} %fusion.50) | copy-start | bytes 12292
  155.7 32.4 %copy-start.20 = (s32[1024]{0:T(1024)S(1)}, s32[1024]{0:T(1024)}, u32[]{:S(2)}) copy-start(s32[1024]{0:T(1024)} %broadcast_clamp_fusion) | copy-start | bytes 12292
  194.8 12.9 %all-to-all-start.1 = ((bf16[2,2,98304]{2,1,0:T(2,128)(2,1)}), bf16[2,2,98304]{2,1,0:T(2,128)(2,1)}, u32[]{:S(2)}, u32[]{:S(2)}) async-start(bf16[2,2,98304]{2,1,0:T(2,128)(2,1)} %reshape.337), calls=%async_computation.1 | async-start | bytes 1572864 | tf_op jit(solution)/shard_map/all_to_all | solution.py:140
  276.5 12.6 %all-to-all-start.2 = ((bf16[512,2,384]{2,0,1:T(8,128)(2,1)}), bf16[512,2,384]{2,0,1:T(8,128)(2,1)S(1)}, u32[]{:S(2)}, u32[]{:S(2)}) async-start(bf16[512,2,384]{2,0,1:T(8,128)(2,1)} %bitcast.160), calls=%async_computation.2 | async-start | bytes 1572864 | tf_op jit(solution)/shard_map/all_to_all | solution.py:200
  280.1 281.2 %all-reduce.25.cloned.1.call-start = ((), (), s32[]{:S(2)}) async-start(), calls=%async_computation.17 | async-start | bytes 21233664 | tf_op jit(solution)/shard_map/psum | solution.py:278
  289.0 362.9 %all-gather.15.cloned.1.call-start = ((), (), s32[]{:S(2)}) async-start(), calls=%async_computation.15 | async-start | bytes 10616832 | tf_op jit(solution)/shard_map/all_gather | solution.py:277
  458.0 428.9 %reduce-scatter.7.cloned.1.call-start = ((), (), s32[]{:S(2)}) async-start(), calls=%async_computation.12 | async-start | bytes 2506752 | tf_op jit(solution)/shard_map/reduce_scatter | solution.py:293
  564.1 322.7 %reduce-scatter.13.cloned.1.call-start = ((), (), s32[]{:S(2)}) async-start(), calls=%async_computation.16 | async-start | bytes 7520256
  746.4 206.1 %reduce-scatter.9.cloned.1.call-start = ((), (), s32[]{:S(2)}) async-start(), calls=%async_computation.13 | async-start | bytes 10027008 | tf_op jit(solution)/shard_map/reduce_scatter | solution.py:294
  754.0 313.8 %reduce-scatter.11.cloned.1.call-start = ((), (), s32[]{:S(2)}) async-start(), calls=%async_computation.14 | async-start | bytes 10027008 | tf_op jit(solution)/shard_map/reduce_scatter | solution.py:295
  761.6 46.5 %copy-start.6 = (bf16[512,3,2,1,384]{0,4,2,1,3:T(8,128)(2,1)S(1)}, bf16[512,3,2,1,384]{0,4,2,1,3:T(8,128)(2,1)}, u32[]{:S(2)}) copy-start(bf16[512,3,2,1,384]{0,4,2,1,3:T(8,128)(2,1)} %copy.117) | copy-start | bytes 7077892
  761.6 46.8 %copy-start.28 = (bf16[768]{0:T(1024)(128)(2,1)S(1)}, bf16[768]{0:T(1024)(128)(2,1)}, u32[]{:S(2)}) copy-start(bf16[768]{0:T(1024)(128)(2,1)} %get-tuple-element.544) | copy-start | bytes 4612
  761.6 46.8 %copy-start.29 = (bf16[768]{0:T(1024)(128)(2,1)S(1)}, bf16[768]{0:T(1024)(128)(2,1)}, u32[]{:S(2)}) copy-start(bf16[768]{0:T(1024)(128)(2,1)} %get-tuple-element.546) | copy-start | bytes 4612
  761.6 46.8 %copy-start.30 = (bf16[768]{0:T(1024)(128)(2,1)S(1)}, bf16[768]{0:T(1024)(128)(2,1)}, u32[]{:S(2)}) copy-start(bf16[768]{0:T(1024)(128)(2,1)} %get-tuple-element.627) | copy-start | bytes 4612
  761.7 46.8 %copy-start.31 = (bf16[768]{0:T(1024)(128)(2,1)S(1)}, bf16[768]{0:T(1024)(128)(2,1)}, u32[]{:S(2)}) copy-start(bf16[768]{0:T(1024)(128)(2,1)} %get-tuple-element.631) | copy-start | bytes 4612
  761.7 46.8 %copy-start.32 = (bf16[3072]{0:T(1024)(128)(2,1)S(1)}, bf16[3072]{0:T(1024)(128)(2,1)}, u32[]{:S(2)}) copy-start(bf16[3072]{0:T(1024)(128)(2,1)} %get-tuple-element.629) | copy-start | bytes 18436
  761.7 46.8 %copy-start.40 = (bf16[768]{0:T(1024)(128)(2,1)S(1)}, bf16[768]{0:T(1024)(128)(2,1)}, u32[]{:S(2)}) copy-start(bf16[768]{0:T(1024)(128)(2,1)} %get-tuple-element.533) | copy-start | bytes 4612
  761.7 46.8 %copy-start.41 = (bf16[768]{0:T(1024)(128)(2,1)S(1)}, bf16[768]{0:T(1024)(128)(2,1)}, u32[]{:S(2)}) copy-start(bf16[768]{0:T(1024)(128)(2,1)} %get-tuple-element.539) | copy-start | bytes 4612
  761.7 119.7 %copy-start.27 = (f32[512]{0:T(512)S(1)}, f32[512]{0:T(512)}, u32[]{:S(2)}) copy-start(f32[512]{0:T(512)} %copy-done.26) | copy-start | bytes 6148
  (39 other events, 269.4 us)
Sparse Core Ops, SparseCore 0:
  10.3 50.2 all-gather.6
  62.8 36.8 all-gather.8
  102.0 51.9 all-gather.10
  156.1 51.7 all-gather.12
  289.1 272.0 all-reduce.24
  562.7 89.2 all-gather.14
  656.3 63.2 reduce-scatter.6
  746.5 90.4 reduce-scatter.12
  841.7 110.7 reduce-scatter.8
  957.0 110.8 reduce-scatter.10
